TPU v7x, 32 devices: a whole 2x2x4 slice. The times are simulated.
32 devices in a mesh: dp: 4 (over y, core), feat: 8 (over z, x).
Axes of the slice: x: 2, y: 2, z: 4, core: 2. Of those that a mesh axis runs over, the one named last changes fastest.
Arguments:
- images: bfloat16 [1536, 3072], P('dp'), may hold values from -6 to 6
- labels: int32 [1536], P('dp'), may hold values from 0 to 9
- frequencies: bfloat16 [3072, 8192], P(None, 'feat'), may hold values from -0.15625 to 0.15625
- privacy_noise: float32 [10, 2, 8192], P(None, None, 'feat'), may hold values from -0.6 to 0.6
- latents: bfloat16 [1024, 256], P('dp'), may hold values from -6 to 6
- gen_labels: int32 [1024], P('dp'), may hold values from 0 to 9
- gen_in: bfloat16 [256, 1024], replicated, may hold values from -0.375 to 0.375
- gen_out: bfloat16 [1024, 3072], replicated, may hold values from -0.25 to 0.25
Outputs:
- match_loss: float32 [], replicated
- grad_in: float32 [256, 1024], P('dp')
- grad_out: float32 [1024, 3072], P('dp')
All inputs are finite; a program needn't handle non-finite values.
Results may differ from a plain program's by a relative error of at most 0.0035.
Values sent between devices are 32-bit elements; how exact they have to be, the bound alone decides.
No kernel may reach another device: no remote copies, remote signals or barrier semaphores. Data moves between devices by JAX's collectives and lax.ppermute only.
A program may use at most 128 MiB of HBM per device.

v0:
```python
import jax
import jax.numpy as jnp
from jax import lax
from jax.sharding import PartitionSpec as P


def class_sums(phase, classes_of, classes, scale):
    feats = jnp.concatenate([jnp.cos(phase), jnp.sin(phase)], axis=1)
    onehot = (classes_of[:, None] == jnp.arange(classes)[None, :]).astype(jnp.float32)
    sums = jnp.dot(onehot.T, feats, precision=lax.Precision.HIGHEST) * scale
    return (sums.reshape(classes, 2, phase.shape[1]), onehot)


def generator_grads(image_grad, image_out, hidden, pre_hidden, sigmoid_h, latents, gen_out):
    out_grad = (image_grad * (1.0 - image_out * image_out)).astype(jnp.bfloat16)
    grad_out = jnp.einsum("gh,gd->hd", hidden, out_grad, preferred_element_type=jnp.float32)
    back_hidden = jnp.einsum("gd,hd->gh", out_grad, gen_out, preferred_element_type=jnp.float32)
    hidden_grad = (back_hidden * sigmoid_h * (1.0 + pre_hidden * (1.0 - sigmoid_h))).astype(
        jnp.bfloat16
    )
    grad_in = jnp.einsum("gz,gh->zh", latents, hidden_grad, preferred_element_type=jnp.float32)
    return (grad_in, grad_out)


def per_device(images, labels, frequencies, privacy_noise, latents, gen_labels, gen_in, gen_out):
    classes = privacy_noise.shape[0]
    feat_dev = frequencies.shape[1]
    data_devices = lax.axis_size("dp")
    feat_devices = lax.axis_size("feat")
    total_images = images.shape[0] * data_devices
    total_gen = latents.shape[0] * data_devices
    total_feats = feat_dev * feat_devices
    data_phase = jnp.dot(images, frequencies, preferred_element_type=jnp.float32)
    data_part, unused = class_sums(data_phase, labels, classes, classes / total_images)
    pre_hidden = jnp.dot(latents, gen_in, preferred_element_type=jnp.float32)
    sigmoid_h = jax.nn.sigmoid(pre_hidden)
    hidden = (pre_hidden * sigmoid_h).astype(jnp.bfloat16)
    image_out = jnp.tanh(jnp.dot(hidden, gen_out, preferred_element_type=jnp.float32))
    gen_image = image_out.astype(jnp.bfloat16)
    gen_phase = jnp.dot(gen_image, frequencies, preferred_element_type=jnp.float32)
    gen_part, gen_onehot = class_sums(gen_phase, gen_labels, classes, classes / total_gen)
    mean_gap = lax.psum(gen_part - data_part, "dp") - privacy_noise
    match_loss = lax.psum(jnp.sum(mean_gap * mean_gap), "feat") / (2.0 * total_feats)
    gap_rows = jnp.dot(
        gen_onehot, mean_gap.reshape(classes, 2 * feat_dev), precision=lax.Precision.HIGHEST
    ) * (16.0 * classes / total_gen)
    phase_grad = (
        jnp.cos(gen_phase) * gap_rows[:, feat_dev:] - jnp.sin(gen_phase) * gap_rows[:, :feat_dev]
    ).astype(jnp.bfloat16)
    partial_image = jnp.einsum(
        "gf,df->gd", phase_grad, frequencies, preferred_element_type=jnp.float32
    )
    image_grad = lax.psum(partial_image, "feat")
    grad_in, grad_out = generator_grads(
        image_grad, image_out, hidden, pre_hidden, sigmoid_h, latents, gen_out
    )
    grad_in, grad_out = (
        lax.psum_scatter(grad_in, "dp", scatter_dimension=0, tiled=True),
        lax.psum_scatter(grad_out, "dp", scatter_dimension=0, tiled=True),
    )
    return (match_loss, grad_in, grad_out)


def solution(mesh):
    return jax.shard_map(
        per_device,
        mesh=mesh,
        in_specs=(
            P("dp", None),
            P("dp"),
            P(None, "feat"),
            P(None, None, "feat"),
            P("dp", None),
            P("dp"),
            P(),
            P(),
        ),
        out_specs=(P(), P("dp", None), P("dp", None)),
        check_vma=False,
    )
```

profile of v0, /device:TPU:0, one launch (start us, length us, event | category | flops | bytes accessed | tf_op | source)
XLA Modules:
  0.0 356.0 jit_solution(9388458838005756762)
XLA Ops:
  7.2 0.0 all-reduce.3.cloned.1.call-start
  7.2 1.6 fusion.34
  8.8 1.0 copy-done.4
  9.8 4.8 %convolution_tanh_fusion = f32[256,3072]{1,0:T(8,128)S(1)} fusion(bf16[1024,3072]{1,0:T(8,128)(2,1)} %param.15, f32[256,1024]{1,0:T(8,128)S(1)} %fusion.34), kind=kOutput, calls=%fused_computation | convolution fusion | flops 1611923456 | bytes 10485760 | tf_op jit(solution)/shard_map/dot_general | solution.py:38
  14.6 5.3 %fusion.33 = (f32[256,1024]{1,0:T(8,128)S(1)}, f32[256,1024]{1,0:T(8,128)S(1)}) fusion(bf16[3072,1024]{1,0:T(8,128)(2,1)S(1)} %bitcast.19, f32[256,3072]{1,0:T(8,128)S(1)} %convolution_tanh_fusion), kind=kOutput, calls=%fused_computation.41 | convolution fusion | flops 1611399168 | bytes 11534336 | tf_op jit(solution)/shard_map/dot_general | solution.py:40
  20.0 12.3 %fusion.32 = (f32[384,1024]{1,0:T(8,128)S(1)}, f32[384,1024]{1,0:T(8,128)S(1)}) fusion(bf16[384,3072]{1,0:T(8,128)(2,1)S(1)} %copy-done, bf16[3072,1024]{1,0:T(8,128)(2,1)S(1)} %bitcast.19), kind=kOutput, calls=%fused_computation.40 | convolution fusion | flops 2415919104 | bytes 11796480 | tf_op jit(solution)/shard_map/dot_general | solution.py:33
  32.3 0.8 convolution_multiply_fusion.1
  33.1 1.2 fusion.7
  34.3 0.7 sub.22
  35.0 0.2 all-reduce.5.cloned.1.call-start
  35.3 32.9 %all-reduce.3.cloned.1.call-done = f32[10,2,1024]{2,1,0:T(2,128)} async-done(((f32[10,2,1024]{2,1,0:T(2,128)}), f32[10,2,1024]{2,1,0:T(2,128)}) %all-reduce.3.cloned.1.call-update) | async-done | bytes 81936 | tf_op jit(solution)/shard_map/psum | solution.py:42
  68.2 1.7 multiply_reduce_fusion
  70.0 1.0 convolution_multiply_fusion
  71.0 6.4 %fusion.22 = f32[256,3072]{1,0:T(8,128)} fusion(bf16[3072,1024]{1,0:T(8,128)(2,1)} %param.10, f32[256,1024]{1,0:T(8,128)S(1)} %copy-done.3, f32[256,2048]{1,0:T(8,128)S(1)} %convolution_multiply_fusion, f32[256,1024]{1,0:T(8,128)S(1)} %get-tuple-element.13), kind=kOutput, calls=%fused_computation.28 | convolution fusion | flops 1611661312 | bytes 13631488 | tf_op jit(solution)/shard_map/gf,df->gd/dot_general | solution.py:50
  77.5 0.0 reduce-scatter.7.cloned.1.call-start
  77.5 130.2 %all-reduce.5.cloned.1.call-done = f32[256,3072]{1,0:T(8,128)} async-done(((f32[256,3072]{1,0:T(8,128)}), f32[256,3072]{1,0:T(8,128)}) %all-reduce.5.cloned.1.call-update) | async-done | bytes 3145744 | tf_op jit(solution)/shard_map/psum | solution.py:53
  207.7 4.6 %multiply_convert_fusion = bf16[256,3072]{1,0:T(8,128)(2,1)} fusion(f32[256,3072]{1,0:T(8,128)} %all-reduce.5.cloned.1.call-done, f32[256,3072]{1,0:T(8,128)} %copy-done.1), kind=kLoop, calls=%fused_computation.5 | loop fusion | flops 3145728 | bytes 7864320 | tf_op jit(solution)/shard_map/convert_element_type | solution.py:15
  212.3 6.6 %convolution_bitcast_fusion = f32[256,1024]{0,1:T(8,128)} fusion(bf16[256,256]{1,0:T(8,128)(2,1)S(1)} %copy-done.6, bf16[256,3072]{1,0:T(8,128)(2,1)} %multiply_convert_fusion, bf16[1024,3072]{1,0:T(8,128)(2,1)} %param.15, f32[256,1024]{1,0:T(8,128)S(1)} %copy-done.5), kind=kOutput, calls=%fused_computation.17 | convolution fusion | flops 1747189760 | bytes 10092544 | tf_op jit(solution)/shard_map/gz,gh->zh/dot_general | solution.py:21
  218.9 2.6 copy.13
  221.5 0.0 reduce-scatter.5.cloned.1.call-start
  221.5 8.0 %fusion.31 = f32[1024,3072]{1,0:T(8,128)} fusion(bf16[256,3072]{1,0:T(8,128)(2,1)} %multiply_convert_fusion, f32[256,1024]{1,0:T(8,128)S(1)} %copy-done.5), kind=kOutput, calls=%fused_computation.39 | convolution fusion | flops 1611923456 | bytes 15204352 | tf_op jit(solution)/shard_map/gh,gd->hd/dot_general | solution.py:16
  229.6 19.9 %psum.22 = f32[]{:T(128)} all-reduce(f32[]{:T(128)} %get-tuple-element.9), channel_id=1, replica_groups=mesh['dp'=4,'feat'=8] {'feat'}, use_global_device_ids=true, to_apply=%region_2.0 | all-reduce | flops 1 | bytes 8 | tf_op jit(solution)/shard_map/psum | solution.py:43
  250.1 0.0 reduce-scatter.7.cloned.1.call-done
  250.1 98.3 %reduce-scatter.5.cloned.1.call-done = f32[256,3072]{1,0:T(8,128)} async-done(((f32[1024,3072]{1,0:T(8,128)}), f32[256,3072]{1,0:T(8,128)}) %reduce-scatter.5.cloned.1.call-update) | async-done | bytes 3145744 | tf_op jit(solution)/shard_map/reduce_scatter | solution.py:59
  (28 shorter events, 0.2 us)
Async XLA Ops:
  7.2 12.8 %copy-start = (bf16[384,3072]{1,0:T(8,128)(2,1)S(1)}, bf16[384,3072]{1,0:T(8,128)(2,1)}, u32[]{:S(2)}) copy-start(bf16[384,3072]{1,0:T(8,128)(2,1)} %param.8) | copy-start | bytes 7077892
  7.2 61.0 %all-reduce.3.cloned.1.call-start = ((), (), s32[]{:S(2)}) async-start(), calls=%async_computation.2 | async-start | bytes 163840 | tf_op jit(solution)/shard_map/psum | solution.py:42
  7.2 7.4 %slice-start = ((s8[6291456]{0:T(1024)(128)(4,1)}), s8[4194304]{0:T(1024)(128)(4,1)S(1)}, s32[]{:S(2)}) async-start(s8[6291456]{0:T(1024)(128)(4,1)} %bitcast.18), calls=%async_computation.6 | async-start | bytes 8388608
  8.8 1.0 copy-start.4
  9.8 4.8 %slice-start.1 = ((s8[6291456]{0:T(1024)(128)(4,1)}), s8[2097152]{0:T(1024)(128)(4,1)S(1)}, s32[]{:S(2)}) async-start(s8[6291456]{0:T(1024)(128)(4,1)} %bitcast.18), calls=%async_computation.7 | async-start | bytes 4194304
  14.6 5.3 %copy-start.1 = (f32[256,3072]{1,0:T(8,128)}, f32[256,3072]{1,0:T(8,128)S(1)}, u32[]{:S(2)}) copy-start(f32[256,3072]{1,0:T(8,128)S(1)} %convolution_tanh_fusion) | copy-start | bytes 9437188
  20.0 12.3 %copy-start.2 = (f32[256,1024]{1,0:T(8,128)}, f32[256,1024]{1,0:T(8,128)S(1)}, u32[]{:S(2)}) copy-start(f32[256,1024]{1,0:T(8,128)S(1)} %get-tuple-element.14) | copy-start | bytes 3145732
  20.0 12.3 %copy-start.7 = (s32[256]{0:T(256)S(1)}, s32[256]{0:T(256)}, u32[]{:S(2)}) copy-start(s32[256]{0:T(256)} %param.13) | copy-start | bytes 3076
  20.0 13.2 %copy-start.8 = (s32[384]{0:T(512)S(1)}, s32[384]{0:T(512)}, u32[]{:S(2)}) copy-start(s32[384]{0:T(512)} %param.9) | copy-start | bytes 4612
  35.0 172.7 %all-reduce.5.cloned.1.call-start = ((), (), s32[]{:S(2)}) async-start(), calls=%async_computation.3 | async-start | bytes 6291456 | tf_op jit(solution)/shard_map/psum | solution.py:53
  68.2 2.8 copy-start.3
  77.5 134.8 %copy-start.5 = (f32[256,1024]{1,0:T(8,128)S(1)}, f32[256,1024]{1,0:T(8,128)}, u32[]{:S(2)}) copy-start(f32[256,1024]{1,0:T(8,128)} %copy-done.4) | copy-start | bytes 3145732
  77.5 134.8 %copy-start.6 = (bf16[256,256]{1,0:T(8,128)(2,1)S(1)}, bf16[256,256]{1,0:T(8,128)(2,1)}, u32[]{:S(2)}) copy-start(bf16[256,256]{1,0:T(8,128)(2,1)} %param.12) | copy-start | bytes 393220
  77.5 172.6 %reduce-scatter.7.cloned.1.call-start = ((), (), s32[]{:S(2)}) async-start(), calls=%async_computation.5 | async-start | bytes 1310720
  221.5 126.9 %reduce-scatter.5.cloned.1.call-start = ((), (), s32[]{:S(2)}) async-start(), calls=%async_computation.4 | async-start | bytes 15728640 | tf_op jit(solution)/shard_map/reduce_scatter | solution.py:59
Sparse Core Ops, SparseCore 0:
  35.2 32.9 all-reduce.2
  77.6 130.0 all-reduce.4
  221.6 23.8 reduce-scatter.6
  248.5 99.8 reduce-scatter.4
where the time goes:
time: 356 us
  waiting for transfers between devices  261 us (73%)
  matrix products  47.9 us (13%)
  blocking collectives  19.9 us (6%)
  between operations  15.7 us (4%)
  other arithmetic  6.29 us (2%)
  local copies, waits for them, and re-layouts  4.46 us (1%)
    psum x1, waiting for transfers between devices, per_device(): image_grad = lax.psum(partial_image, 'feat')  130 us
    reduce_scatter x1, waiting for transfers between devices, per_device(): lax.psum_scatter(grad_out, 'dp', scatter_dimension=0, tiled=True)  98.3 us
    psum x1, waiting for transfers between devices, per_device(): mean_gap = lax.psum(gen_part - data_part, 'dp') - privacy_noise  32.9 us
    psum x1, blocking collectives, per_device(): lax.psum(jnp.sum(mean_gap * mean_gap), 'feat') / (2.0 * total_feats)  19.9 us
    dot_general x1, matrix products, per_device(): jnp.dot(images, frequencies, preferred_element_type=jnp.float32)  12.3 us
    dot_general x1, matrix products, generator_grads(): jnp.einsum('gh,gd->hd', hidden, out_grad, preferred_element_type=jnp.floa...  8.02 us
  transfers between devices with their start and end apart: 4, of which 3 were waited for; matrix products, arithmetic and copies ran while one was open for 2% of the time, Pallas kernels for 0%

commit v1 on v0

--- a/solution.py
+++ b/solution.py
@@ -2,6 +2,15 @@
 import jax.numpy as jnp
 from jax import lax
 from jax.sharding import PartitionSpec as P
+
+
+def added_up(x, axis):
+    n_dev = lax.axis_size(axis)
+    summed, stride = (x, 1)
+    while stride < n_dev:
+        summed = summed + lax.ppermute(summed, axis, [(i, i ^ stride) for i in range(n_dev)])
+        stride = 2 * stride
+    return summed
 
 
 def class_sums(phase, classes_of, classes, scale):
@@ -50,7 +59,7 @@
     partial_image = jnp.einsum(
         "gf,df->gd", phase_grad, frequencies, preferred_element_type=jnp.float32
     )
-    image_grad = lax.psum(partial_image, "feat")
+    image_grad = added_up(partial_image, "feat")
     grad_in, grad_out = generator_grads(
         image_grad, image_out, hidden, pre_hidden, sigmoid_h, latents, gen_out
     )

time: 356 us -> 500 us (1.40)
  waiting for transfers between devices: 261 us -> 400 us
  starting transfers between devices: 0.35 us -> 6.38 us
    ppermute x0 -> x3, waiting for transfers between devices: none -> 270 us  [added_up(): lax.ppermute(summed, axis, [(i, i ^ stride) for i in range(n_dev)])]
    psum x1 -> x0, waiting for transfers between devices: 130 us -> none  [per_device(): image_grad = lax.psum(partial_image, 'feat')]
    ppermute x0 -> x3, starting transfers between devices: none -> 6.08 us  [added_up(): lax.ppermute(summed, axis, [(i, i ^ stride) for i in range(n_dev)])]
  transfers between devices with their start and end apart: 4 -> 6, of which waited for: 3 -> 5; matrix products, arithmetic and copies ran while one was open for 2% -> 2% of each run, Pallas kernels for 0% -> 0%
where the time goes in v1:
time: 500 us
  waiting for transfers between devices  400 us (80%)
  matrix products  46.2 us (9%)
  blocking collectives  22.2 us (4%)
  between operations  15.8 us (3%)
  starting transfers between devices  6.38 us (1%)
    ppermute x3, waiting for transfers between devices, added_up(): lax.ppermute(summed, axis, [(i, i ^ stride) for i in range(n_dev)])  270 us
    reduce_scatter x1, waiting for transfers between devices, per_device(): lax.psum_scatter(grad_out, 'dp', scatter_dimension=0, tiled=True)  97.1 us
    psum x1, waiting for transfers between devices, per_device(): mean_gap = lax.psum(gen_part - data_part, 'dp') - privacy_noise  32.9 us
    psum x1, blocking collectives, per_device(): lax.psum(jnp.sum(mean_gap * mean_gap), 'feat') / (2.0 * total_feats)  22.2 us
    dot_general x1, matrix products, per_device(): jnp.dot(images, frequencies, preferred_element_type=jnp.float32)  12.3 us
  transfers between devices with their start and end apart: 6, of which 5 were waited for; matrix products, arithmetic and copies ran while one was open for 2% of the time, Pallas kernels for 0%

profile of v1, /device:TPU:0, one launch (start us, length us, event | category | flops | bytes accessed | tf_op | source)
XLA Modules:
  0.0 499.8 jit_solution(3305933044144210588)
XLA Ops:
  7.2 1.6 fusion.34
  8.8 1.0 copy-done.5
  9.8 4.8 convolution_tanh_fusion
  14.6 5.3 %fusion.33 = (f32[256,1024]{1,0:T(8,128)S(1)}, f32[256,1024]{1,0:T(8,128)S(1)}) fusion(bf16[3072,1024]{1,0:T(8,128)(2,1)S(1)} %bitcast.19, f32[256,3072]{1,0:T(8,128)S(1)} %convolution_tanh_fusion), kind=kOutput, calls=%fused_computation.41 | convolution fusion | flops 1611399168 | bytes 11534336 | tf_op jit(solution)/shard_map/dot_general | solution.py:49
  20.0 12.3 %fusion.32 = (f32[384,1024]{1,0:T(8,128)S(1)}, f32[384,1024]{1,0:T(8,128)S(1)}) fusion(bf16[384,3072]{1,0:T(8,128)(2,1)S(1)} %copy-done, bf16[3072,1024]{1,0:T(8,128)(2,1)S(1)} %bitcast.19), kind=kOutput, calls=%fused_computation.40 | convolution fusion | flops 2415919104 | bytes 11796480 | tf_op jit(solution)/shard_map/dot_general | solution.py:42
  32.3 0.8 convolution_multiply_fusion.1
  33.1 1.2 fusion.7
  34.3 0.7 sub.22
  35.2 32.9 %all-reduce.2.cloned.1.call-done = f32[10,2,1024]{2,1,0:T(2,128)} async-done(((f32[10,2,1024]{2,1,0:T(2,128)}), f32[10,2,1024]{2,1,0:T(2,128)}) %all-reduce.2.cloned.1.call-update) | async-done | bytes 81936 | tf_op jit(solution)/shard_map/psum | solution.py:51
  68.2 1.7 multiply_reduce_fusion
  70.0 1.0 convolution_multiply_fusion
  71.0 4.8 fusion.22
  75.8 1.5 collective-permute-start
  77.3 68.4 %collective-permute-done = f32[256,3072]{1,0:T(8,128)S(1)} collective-permute-done((f32[256,3072]{1,0:T(8,128)S(1)}, f32[256,3072]{1,0:T(8,128)S(1)}, u32[]{:S(2)}, u32[]{:S(2)}) %collective-permute-start) | collective-permute-done | bytes 3145760 | tf_op jit(solution)/shard_map/ppermute | solution.py:11
  146.3 1.8 collective-permute-start.1
  148.1 67.6 %collective-permute-done.1 = f32[256,3072]{1,0:T(8,128)S(1)} collective-permute-done((f32[256,3072]{1,0:T(8,128)S(1)}, f32[256,3072]{1,0:T(8,128)S(1)}, u32[]{:S(2)}, u32[]{:S(2)}) %collective-permute-start.1) | collective-permute-done | bytes 3145760 | tf_op jit(solution)/shard_map/ppermute | solution.py:11
  216.0 2.7 collective-permute-start.2
  218.8 134.1 %collective-permute-done.2 = f32[256,3072]{1,0:T(8,128)S(1)} collective-permute-done((f32[256,3072]{1,0:T(8,128)S(1)}, f32[256,3072]{1,0:T(8,128)S(1)}, u32[]{:S(2)}, u32[]{:S(2)}) %collective-permute-start.2) | collective-permute-done | bytes 3145760 | tf_op jit(solution)/shard_map/ppermute | solution.py:11
  352.9 2.1 multiply_convert_fusion
  355.0 6.6 %convolution_bitcast_fusion = f32[256,1024]{0,1:T(8,128)} fusion(bf16[256,256]{1,0:T(8,128)(2,1)S(1)} %copy-done.7, bf16[256,3072]{1,0:T(8,128)(2,1)} %multiply_convert_fusion, bf16[1024,3072]{1,0:T(8,128)(2,1)} %param.15, f32[256,1024]{1,0:T(8,128)S(1)} %copy-done.6), kind=kOutput, calls=%fused_computation.17 | convolution fusion | flops 1747189760 | bytes 10092544 | tf_op jit(solution)/shard_map/gz,gh->zh/dot_general | solution.py:30
  361.6 2.6 copy.13
  364.3 7.9 %fusion.31 = f32[1024,3072]{1,0:T(8,128)} fusion(bf16[256,3072]{1,0:T(8,128)(2,1)} %multiply_convert_fusion, f32[256,1024]{1,0:T(8,128)S(1)} %copy-done.6), kind=kOutput, calls=%fused_computation.39 | convolution fusion | flops 1611923456 | bytes 15204352 | tf_op jit(solution)/shard_map/gh,gd->hd/dot_general | solution.py:25
  372.3 22.2 %psum.15 = f32[]{:T(128)} all-reduce(f32[]{:T(128)} %get-tuple-element.9), channel_id=1, replica_groups=mesh['dp'=4,'feat'=8] {'feat'}, use_global_device_ids=true, to_apply=%region_2.0 | all-reduce | flops 1 | bytes 8 | tf_op jit(solution)/shard_map/psum | solution.py:52
  395.1 97.1 %reduce-scatter.5.cloned.1.call-done = f32[256,3072]{1,0:T(8,128)} async-done(((f32[1024,3072]{1,0:T(8,128)}), f32[256,3072]{1,0:T(8,128)}) %reduce-scatter.5.cloned.1.call-update) | async-done | bytes 3145744 | tf_op jit(solution)/shard_map/reduce_scatter | solution.py:68
  (35 shorter events, 1.4 us)
Async XLA Ops:
  7.2 12.8 %copy-start = (bf16[384,3072]{1,0:T(8,128)(2,1)S(1)}, bf16[384,3072]{1,0:T(8,128)(2,1)}, u32[]{:S(2)}) copy-start(bf16[384,3072]{1,0:T(8,128)(2,1)} %param.8) | copy-start | bytes 7077892
  7.2 61.0 %all-reduce.2.cloned.1.call-start = ((), (), s32[]{:S(2)}) async-start(), calls=%async_computation.2 | async-start | bytes 163840 | tf_op jit(solution)/shard_map/psum | solution.py:51
  7.2 7.3 %slice-start = ((s8[6291456]{0:T(1024)(128)(4,1)}), s8[4194304]{0:T(1024)(128)(4,1)S(1)}, s32[]{:S(2)}) async-start(s8[6291456]{0:T(1024)(128)(4,1)} %bitcast.18), calls=%async_computation.5 | async-start | bytes 8388608
  8.8 1.0 copy-start.5
  9.8 4.8 slice-start.1
  14.6 5.3 %copy-start.1 = (f32[256,3072]{1,0:T(8,128)}, f32[256,3072]{1,0:T(8,128)S(1)}, u32[]{:S(2)}) copy-start(f32[256,3072]{1,0:T(8,128)S(1)} %convolution_tanh_fusion) | copy-start | bytes 9437188
  19.9 12.3 %copy-start.3 = (f32[256,1024]{1,0:T(8,128)}, f32[256,1024]{1,0:T(8,128)S(1)}, u32[]{:S(2)}) copy-start(f32[256,1024]{1,0:T(8,128)S(1)} %get-tuple-element.14) | copy-start | bytes 3145732
  19.9 12.3 %copy-start.8 = (s32[256]{0:T(256)S(1)}, s32[256]{0:T(256)}, u32[]{:S(2)}) copy-start(s32[256]{0:T(256)} %param.13) | copy-start | bytes 3076
  20.0 13.1 %copy-start.9 = (s32[384]{0:T(512)S(1)}, s32[384]{0:T(512)}, u32[]{:S(2)}) copy-start(s32[384]{0:T(512)} %param.9) | copy-start | bytes 4612
  35.0 360.1 %reduce-scatter.7.cloned.1.call-start = ((), (), s32[]{:S(2)}) async-start(), calls=%async_computation.4 | async-start | bytes 1310720
  68.2 2.8 copy-start.4
  75.8 70.0 %collective-permute-start = (f32[256,3072]{1,0:T(8,128)S(1)}, f32[256,3072]{1,0:T(8,128)S(1)}, u32[]{:S(2)}, u32[]{:S(2)}) collective-permute-start(f32[256,3072]{1,0:T(8,128)S(1)} %fusion.22), channel_id=1, source_target_pairs={{0,1},{1,0},{2,3},{3,2},{4,5},{5,4},{6,7},{7,6},{8,9},{9,8},{10,11... | collective-permute-start | bytes 9437192 | tf_op jit(solution)/shard_map/ppermute | solution.py:11
  146.2 206.7 %copy-start.2 = (f32[256,3072]{1,0:T(8,128)S(1)}, f32[256,3072]{1,0:T(8,128)}, u32[]{:S(2)}) copy-start(f32[256,3072]{1,0:T(8,128)} %copy-done.1) | copy-start | bytes 9437188
  146.3 69.4 %collective-permute-start.1 = (f32[256,3072]{1,0:T(8,128)S(1)}, f32[256,3072]{1,0:T(8,128)S(1)}, u32[]{:S(2)}, u32[]{:S(2)}) collective-permute-start(f32[256,3072]{1,0:T(8,128)S(1)} %add.24), channel_id=1, source_target_pairs={{0,2},{1,3},{2,0},{3,1},{4,6},{5,7},{6,4},{7,5},{8,10},{9,11},{10,... | collective-permute-start | bytes 9437192 | tf_op jit(solution)/shard_map/ppermute | solution.py:11
  216.0 139.0 %copy-start.6 = (f32[256,1024]{1,0:T(8,128)S(1)}, f32[256,1024]{1,0:T(8,128)}, u32[]{:S(2)}) copy-start(f32[256,1024]{1,0:T(8,128)} %copy-done.5) | copy-start | bytes 3145732
  216.0 139.0 %copy-start.7 = (bf16[256,256]{1,0:T(8,128)(2,1)S(1)}, bf16[256,256]{1,0:T(8,128)(2,1)}, u32[]{:S(2)}) copy-start(bf16[256,256]{1,0:T(8,128)(2,1)} %param.12) | copy-start | bytes 393220
  216.0 136.9 %collective-permute-start.2 = (f32[256,3072]{1,0:T(8,128)S(1)}, f32[256,3072]{1,0:T(8,128)S(1)}, u32[]{:S(2)}, u32[]{:S(2)}) collective-permute-start(f32[256,3072]{1,0:T(8,128)S(1)} %add.25), channel_id=1, source_target_pairs={{0,4},{1,5},{2,6},{3,7},{4,0},{5,1},{6,2},{7,3},{8,12},{9,13},{10,... | collective-permute-start | bytes 9437192 | tf_op jit(solution)/shard_map/ppermute | solution.py:11
  364.2 127.9 %reduce-scatter.5.cloned.1.call-start = ((), (), s32[]{:S(2)}) async-start(), calls=%async_computation.3 | async-start | bytes 15728640 | tf_op jit(solution)/shard_map/reduce_scatter | solution.py:68
Sparse Core Ops, SparseCore 0:
  35.1 32.9 all-reduce.1
  364.4 24.9 reduce-scatter.6
  392.5 99.6 reduce-scatter.4
